TPU v7x, 128 devices: a whole 4x4x4 slice. The times are simulated.
128 devices in a mesh: grp: 8 (over x_hi, y), dom: 16 (over z, x_lo, core).
Axes of the slice: x: 4 (x_hi: 2, x_lo: 2; x = x_hi * 2 + x_lo), y: 4, z: 4, core: 2. Of those that a mesh axis runs over, the one named last changes fastest.
Arguments:
- features: bfloat16 [65536, 1024], P(('grp', 'dom')), may hold values from -6 to 6
- node_order: int32 [65536], P(('grp', 'dom')), may hold values from 0 to 65535, as said below
- block_cols: int32 [512, 16], P(('grp', 'dom')), may hold values from 0 to 63
- block_count: int32 [512], P(('grp', 'dom')), may hold values from 1 to 16, as said below
- block_vals: bfloat16 [512, 16, 128, 128], P(('grp', 'dom')), may hold values from -0.1875 to 0.1875
- weight: bfloat16 [1024, 512], replicated, may hold values from -0.1875 to 0.1875
- cotangent: bfloat16 [65536, 512], P(('grp', 'dom')), may hold values from -12 to 12
Outputs:
- hidden: bfloat16 [65536, 512], P(('grp', 'dom'))
- grad_weight: float32 [1024, 512], replicated
Inputs may be any that keep to these rules, and one draw needn't show every extreme that they name: `node_order`: A permutation of the crawl rows; the positions of one device's block of 512 take exactly 4 crawl rows from each device's block of 512 crawl rows. `block_count`: some row of blocks holds exactly 16 live blocks.
All inputs are finite; a program needn't handle non-finite values.
Results may differ from a plain program's by a relative error of at most 0.014.
Values may be sent and summed in bfloat16 or wider, within the bound.
A program may use at most 128 MiB of HBM per device.

v0:
```python
import jax
import jax.numpy as jnp
from jax import lax
from jax.sharding import PartitionSpec as P


def silu_slope(values):
    sig = jax.nn.sigmoid(values)
    return sig * (1.0 + values * (1.0 - sig))


def regroup(features, node_order):
    row_count, width_in = features.shape
    devices = lax.axis_size("grp") * lax.axis_size("dom")
    per_pair = row_count // devices
    source_device = node_order // row_count
    source_row = node_order % row_count
    ordering = jnp.argsort(source_device, stable=True)
    requests = source_row[ordering].reshape(devices, per_pair)
    asked_rows = lax.all_to_all(requests, ("grp", "dom"), split_axis=0, concat_axis=0, tiled=True)
    outgoing = features[asked_rows.reshape(-1)].reshape(devices, per_pair, width_in)
    arrived = lax.all_to_all(outgoing, ("grp", "dom"), split_axis=0, concat_axis=0, tiled=True)
    arrived = arrived.reshape(row_count, width_in)
    inverse = jnp.argsort(ordering)
    return arrived[inverse]


def shards(features, node_order, block_cols, block_count, block_vals, weight, cotangent):
    row_count, width_in = features.shape
    hidden_units = weight.shape[1]
    tiles_dev, blocks, tile_size, _ = block_vals.shape
    ordered = regroup(features, node_order)
    everyone = lax.all_gather(ordered, "dom", axis=0, tiled=True)
    panel_tiles = everyone.reshape(-1, tile_size, width_in)
    live_mask = lax.broadcasted_iota(jnp.int32, (tiles_dev, blocks), 1) < block_count[:, None]
    masked_vals = jnp.where(live_mask[:, :, None, None], block_vals, jnp.zeros((), jnp.bfloat16))
    selected = panel_tiles[block_cols]
    mixed = jnp.einsum("tkij,tkjf->tif", masked_vals, selected, preferred_element_type=jnp.float32)
    mixed = mixed.astype(jnp.bfloat16).reshape(row_count, width_in)
    aggregate = jnp.dot(mixed, weight, preferred_element_type=jnp.float32)
    hidden = jax.nn.silu(aggregate).astype(jnp.bfloat16)
    grad_agg = (cotangent.astype(jnp.float32) * silu_slope(aggregate)).astype(jnp.bfloat16)
    local_grad = lax.dot_general(
        mixed, grad_agg, (((0,), (0,)), ((), ())), preferred_element_type=jnp.float32
    )
    grad_weight = lax.psum(local_grad, ("grp", "dom"))
    return (hidden, grad_weight)


def solution(mesh):
    placed = (
        P(("grp", "dom"), None),
        P(("grp", "dom")),
        P(("grp", "dom"), None),
        P(("grp", "dom")),
        P(("grp", "dom"), None, None, None),
        P(),
        P(("grp", "dom"), None),
    )
    return jax.shard_map(
        shards,
        mesh=mesh,
        in_specs=placed,
        out_specs=(P(("grp", "dom"), None), P()),
        check_vma=False,
    )
```

profile of v0, /device:TPU:1, one launch (start us, length us, event | category | flops | bytes accessed | tf_op | source)
XLA Modules:
  0.0 341.9 jit_solution(17413993428679002675)
XLA Ops:
  7.2 0.0 copy-start
  7.2 0.8 add_select_fusion
  8.0 3.8 %sort.34 = (s32[512]{0:T(512)}, s32[512]{0:T(512)S(1)}) sort(s32[512]{0:T(512)S(1)} %get-tuple-element.6, s32[512]{0:T(512)S(1)} %iota.16), dimensions={0}, to_apply=%region_0.1 | sort | flops 4608 | bytes 8192 | tf_op jit(solution)/shard_map/jit(argsort)/sort | solution.py:18
  11.7 3.5 %gather_fusion = s32[512]{0:T(512)S(1)} fusion(s32[512]{0:T(512)S(1)} %get-tuple-element.7, s32[1024]{0:T(1024)S(1)} %pad_clamp_fusion.3), kind=kCustom, calls=%fused_computation | custom fusion | bytes 6144 | tf_op jit(solution)/shard_map/gather | solution.py:19
  15.2 0.1 all_to_all.9
  15.4 20.9 %all_to_all.14 = s32[128,1,4]{2,1,0:T(1,128)S(1)} all-to-all(s32[128,1,4]{2,1,0:T(1,128)S(1)} %bitcast.16), channel_id=1, replica_groups=mesh['grp'=8,'dom'=16] {'grp','dom'}, dimensions={0} | all-to-all | bytes 4096 | tf_op jit(solution)/shard_map/all_to_all | solution.py:20
  36.2 0.5 broadcast.76
  36.7 0.8 reduce.3
  37.6 0.1 reshape.71
  37.7 0.0 copy-done
  37.7 2.1 gather_fusion.1
  39.8 1.2 reshape.72
  41.0 4.4 %all-to-all-start.1 = ((bf16[128,4,1024]{2,1,0:T(4,128)(2,1)}), bf16[128,4,1024]{2,1,0:T(4,128)(2,1)S(1)}, u32[]{:S(2)}, u32[]{:S(2)}) async-start(bf16[128,4,1024]{2,1,0:T(4,128)(2,1)} %reshape.72), calls=%async_computation.1 | async-start | bytes 2097152 | tf_op jit(solution)/shard_map/all_to_all | solution.py:22
  45.4 0.0 all-gather.3.cloned.1.call-start
  45.4 3.8 %sort.35 = (s32[512]{0:T(512)}, s32[512]{0:T(512)S(1)}) sort(s32[512]{0:T(512)S(1)} %get-tuple-element.4, s32[512]{0:T(512)S(1)} %iota.17), dimensions={0}, to_apply=%region_1.2 | sort | flops 4608 | bytes 8192 | tf_op jit(solution)/shard_map/jit(argsort)/sort | solution.py:24
  49.2 15.2 %all-to-all-done.1 = bf16[128,4,1024]{2,1,0:T(4,128)(2,1)S(1)} async-done(((bf16[128,4,1024]{2,1,0:T(4,128)(2,1)}), bf16[128,4,1024]{2,1,0:T(4,128)(2,1)S(1)}, u32[]{:S(2)}, u32[]{:S(2)}) %all-to-all-start.1) | async-done | bytes 1048608 | tf_op jit(solution)/shard_map/all_to_all | solution.py:22
  64.4 0.3 reshape.73
  64.7 0.0 copy-start.2
  64.7 0.0 copy-start.5
  64.7 2.8 gather_fusion.2
  67.5 0.0 all-gather.3.cloned.1.call-update
  67.5 0.0 all-reduce.2.cloned.1.call-start
  67.6 0.0 copy-done.2
  67.6 0.1 reshape.102
  67.7 0.0 copy-done.5
  67.7 0.1 iota_compare_fusion
  67.8 88.4 %all-gather.3.cloned.1.call-done = bf16[8192,1024]{1,0:T(8,128)(2,1)} async-done(((bf16[512,1024]{1,0:T(8,128)(2,1)}), bf16[8192,1024]{1,0:T(8,128)(2,1)}) %all-gather.3.cloned.1.call-update) | async-done | bytes 16777232 | tf_op jit(solution)/shard_map/all_gather | solution.py:33
  156.2 0.0 copy-start.1
  156.2 13.5 %gather_fusion.3 = bf16[64,128,1024]{2,1,0:T(8,128)(2,1)} fusion(bf16[64,128,1024]{2,1,0:T(8,128)(2,1)} %bitcast.13, s32[1024]{0:T(1024)S(1)} %pad_clamp_fusion), kind=kCustom, calls=%fused_computation.3 | custom fusion | bytes 33554688 | tf_op jit(solution)/shard_map/gather | solution.py:37
  169.7 0.0 copy-done.1
  169.7 0.0 copy-start.3
  169.7 7.3 %bitcast_convert_fusion = bf16[4,128,1024]{2,1,0:T(8,128)(2,1)S(1)} fusion(bf16[4,16,128,1024]{3,2,1,0:T(8,128)(2,1)} %bitcast.12, bf16[4,16,128,128]{3,2,1,0:T(8,128)(2,1)S(1)} %copy-done.1, pred[4,16]{1,0:T(4,128)(4,1)S(1)} %iota_compare_fusion), kind=kOutput, calls=%fused_computation.4 | convolution fusion | flops 2149056512 | bytes 19923008 | tf_op jit(solution)/shard_map/tkij,tkjf->tif/dot_general | solution.py:38
  177.0 0.0 copy-done.3
  177.0 0.0 copy-start.4
  177.0 1.6 multiply_convert_fusion.1
  178.7 0.0 copy-done.4
  178.7 2.2 fusion.6
  180.9 0.0 all-reduce.2.cloned.1.call-update
  180.9 151.1 %all-reduce.2.cloned.1.call-done = f32[1024,512]{1,0:T(8,128)} async-done(((f32[1024,512]{1,0:T(8,128)}), f32[1024,512]{1,0:T(8,128)}) %all-reduce.2.cloned.1.call-update) | async-done | bytes 2097168 | tf_op jit(solution)/shard_map/psum | solution.py:46
  332.0 3.1 copy.12
  (10 shorter events, 0.1 us)
Async XLA Ops:
  7.2 30.5 %copy-start = (bf16[512,1024]{1,0:T(8,128)(2,1)S(1)}, bf16[512,1024]{1,0:T(8,128)(2,1)}, u32[]{:S(2)}) copy-start(bf16[512,1024]{1,0:T(8,128)(2,1)} %param.7) | copy-start | bytes 3145732
  41.0 23.5 %all-to-all-start.1 = ((bf16[128,4,1024]{2,1,0:T(4,128)(2,1)}), bf16[128,4,1024]{2,1,0:T(4,128)(2,1)S(1)}, u32[]{:S(2)}, u32[]{:S(2)}) async-start(bf16[128,4,1024]{2,1,0:T(4,128)(2,1)} %reshape.72), calls=%async_computation.1 | async-start | bytes 2097152 | tf_op jit(solution)/shard_map/all_to_all | solution.py:22
  45.4 110.8 %all-gather.3.cloned.1.call-start = ((), (), s32[]{:S(2)}) async-start(), calls=%async_computation.3 | async-start | bytes 17825792 | tf_op jit(solution)/shard_map/all_gather | solution.py:33
  64.7 2.9 copy-start.2
  64.7 3.0 copy-start.5
  67.5 264.5 %all-reduce.2.cloned.1.call-start = ((), (), s32[]{:S(2)}) async-start(), calls=%async_computation.2 | async-start | bytes 4194304 | tf_op jit(solution)/shard_map/psum | solution.py:46
  156.2 13.5 %copy-start.1 = (bf16[4,16,128,128]{3,2,1,0:T(8,128)(2,1)S(1)}, bf16[4,16,128,128]{3,2,1,0:T(8,128)(2,1)}, u32[]{:S(2)}) copy-start(bf16[4,16,128,128]{3,2,1,0:T(8,128)(2,1)} %param.11) | copy-start | bytes 6291460
  169.7 7.3 %copy-start.3 = (bf16[1024,512]{1,0:T(8,128)(2,1)S(1)}, bf16[1024,512]{1,0:T(8,128)(2,1)}, u32[]{:S(2)}) copy-start(bf16[1024,512]{1,0:T(8,128)(2,1)} %param.12) | copy-start | bytes 3145732
  177.0 1.7 copy-start.4
Sparse Core Ops, SparseCore 0:
  67.6 88.4 all-gather.2
  181.1 150.8 all-reduce.1
where the time goes:
time: 342 us
  waiting for transfers between devices  255 us (75%)
  local copies, waits for them, and re-layouts  27.2 us (8%)
  blocking collectives  20.9 us (6%)
  between operations  14.2 us (4%)
  matrix products  11.2 us (3%)
  other arithmetic  9.24 us (3%)
  starting transfers between devices  4.48 us (1%)
    psum x1, waiting for transfers between devices, shards(): grad_weight = lax.psum(local_grad, ('grp', 'dom'))  151 us
    all_gather x1, waiting for transfers between devices, shards(): everyone = lax.all_gather(ordered, 'dom', axis=0, tiled=True)  88.4 us
    all_to_all x1, blocking collectives, regroup(): lax.all_to_all(requests, ('grp', 'dom'), split_axis=0, concat_axis=0, til...  20.9 us
    all_to_all x1, waiting for transfers between devices, regroup(): lax.all_to_all(outgoing, ('grp', 'dom'), split_axis=0, concat_axis=0, til...  15.2 us
    gather x1, local copies, waits for them, and re-layouts, shards(): selected = panel_tiles[block_cols]  13.5 us
    dot_general x1, matrix products, shards(): jnp.einsum('tkij,tkjf->tif', masked_vals, selected, preferred_element_typ...  7.32 us
  transfers between devices with their start and end apart: 3, of which 3 were waited for; matrix products, arithmetic and copies ran while one was open for 1% of the time, Pallas kernels for 0%

commit v1 on v0

--- a/solution.py
+++ b/solution.py
@@ -43,7 +43,7 @@
     local_grad = lax.dot_general(
         mixed, grad_agg, (((0,), (0,)), ((), ())), preferred_element_type=jnp.float32
     )
-    grad_weight = lax.psum(local_grad, ("grp", "dom"))
+    grad_weight = lax.psum(lax.psum(local_grad, "dom"), "grp")
     return (hidden, grad_weight)
 
 

time: 342 us -> 411 us (1.20)
  waiting for transfers between devices: 255 us -> 320 us
    psum x1 -> x2, waiting for transfers between devices: 151 us -> 216 us  [shards(): grad_weight = lax.psum(lax.psum(local_grad, 'dom'), 'grp')]
  transfers between devices with their start and end apart: 3 -> 4, of which waited for: 3 -> 4; matrix products, arithmetic and copies ran while one was open for 1% -> 1% of each run, Pallas kernels for 0% -> 0%
where the time goes in v1:
time: 411 us; the launch traced here: 407 us
  waiting for transfers between devices  320 us (78%)
  local copies, waits for them, and re-layouts  27.2 us (7%)
  blocking collectives  20.9 us (5%)
  between operations  13.9 us (3%)
  matrix products  11.2 us (3%)
  other arithmetic  9.24 us (2%)
  starting transfers between devices  4.52 us (1%)
    psum x2, waiting for transfers between devices, shards(): grad_weight = lax.psum(lax.psum(local_grad, 'dom'), 'grp')  216 us
    all_gather x1, waiting for transfers between devices, shards(): everyone = lax.all_gather(ordered, 'dom', axis=0, tiled=True)  88.4 us
    all_to_all x1, blocking collectives, regroup(): lax.all_to_all(requests, ('grp', 'dom'), split_axis=0, concat_axis=0, til...  20.9 us
    all_to_all x1, waiting for transfers between devices, regroup(): lax.all_to_all(outgoing, ('grp', 'dom'), split_axis=0, concat_axis=0, til...  15.2 us
    gather x1, local copies, waits for them, and re-layouts, shards(): selected = panel_tiles[block_cols]  13.5 us
  transfers between devices with their start and end apart: 4, of which 4 were waited for; matrix products, arithmetic and copies ran while one was open for 1% of the time, Pallas kernels for 0%

profile of v1, /device:TPU:1, one launch (start us, length us, event | category | flops | bytes accessed | tf_op | source)
XLA Modules:
  0.0 406.8 jit_solution(1505442137292094990)
XLA Ops:
  7.2 0.0 copy-start
  7.2 0.8 add_select_fusion
  8.0 3.8 sort.34
  11.7 3.5 gather_fusion
  15.2 0.1 all_to_all.9
  15.4 20.9 %all_to_all.14 = s32[128,1,4]{2,1,0:T(1,128)S(1)} all-to-all(s32[128,1,4]{2,1,0:T(1,128)S(1)} %bitcast.16), channel_id=1, replica_groups=mesh['grp'=8,'dom'=16] {'grp','dom'}, dimensions={0} | all-to-all | bytes 4096 | tf_op jit(solution)/shard_map/all_to_all | solution.py:20
  36.2 0.5 broadcast.76
  36.7 0.8 reduce.3
  37.6 0.1 reshape.71
  37.7 0.0 copy-done
  37.7 2.1 gather_fusion.1
  39.8 1.2 reshape.72
  41.0 4.4 %all-to-all-start.1 = ((bf16[128,4,1024]{2,1,0:T(4,128)(2,1)}), bf16[128,4,1024]{2,1,0:T(4,128)(2,1)S(1)}, u32[]{:S(2)}, u32[]{:S(2)}) async-start(bf16[128,4,1024]{2,1,0:T(4,128)(2,1)} %reshape.72), calls=%async_computation.1 | async-start | bytes 2097152 | tf_op jit(solution)/shard_map/all_to_all | solution.py:22
  45.4 0.0 all-gather.3.cloned.1.call-start
  45.4 3.8 sort.35
  49.2 15.2 %all-to-all-done.1 = bf16[128,4,1024]{2,1,0:T(4,128)(2,1)S(1)} async-done(((bf16[128,4,1024]{2,1,0:T(4,128)(2,1)}), bf16[128,4,1024]{2,1,0:T(4,128)(2,1)S(1)}, u32[]{:S(2)}, u32[]{:S(2)}) %all-to-all-start.1) | async-done | bytes 1048608 | tf_op jit(solution)/shard_map/all_to_all | solution.py:22
  64.4 0.3 reshape.73
  64.7 0.0 copy-start.2
  64.7 0.0 copy-start.5
  64.7 2.8 gather_fusion.2
  67.5 0.0 all-gather.3.cloned.1.call-update
  67.5 0.0 all-reduce.3.cloned.1.call-start
  67.6 0.0 copy-done.2
  67.6 0.1 reshape.102
  67.7 0.0 copy-done.5
  67.7 0.1 iota_compare_fusion
  67.8 88.4 %all-gather.3.cloned.1.call-done = bf16[8192,1024]{1,0:T(8,128)(2,1)} async-done(((bf16[512,1024]{1,0:T(8,128)(2,1)}), bf16[8192,1024]{1,0:T(8,128)(2,1)}) %all-gather.3.cloned.1.call-update) | async-done | bytes 16777232 | tf_op jit(solution)/shard_map/all_gather | solution.py:33
  156.2 0.0 copy-start.1
  156.2 13.5 %gather_fusion.3 = bf16[64,128,1024]{2,1,0:T(8,128)(2,1)} fusion(bf16[64,128,1024]{2,1,0:T(8,128)(2,1)} %bitcast.13, s32[1024]{0:T(1024)S(1)} %pad_clamp_fusion), kind=kCustom, calls=%fused_computation.3 | custom fusion | bytes 33554688 | tf_op jit(solution)/shard_map/gather | solution.py:37
  169.7 0.0 copy-done.1
  169.7 0.0 copy-start.3
  169.7 7.3 %bitcast_convert_fusion = bf16[4,128,1024]{2,1,0:T(8,128)(2,1)S(1)} fusion(bf16[4,16,128,1024]{3,2,1,0:T(8,128)(2,1)} %bitcast.12, bf16[4,16,128,128]{3,2,1,0:T(8,128)(2,1)S(1)} %copy-done.1, pred[4,16]{1,0:T(4,128)(4,1)S(1)} %iota_compare_fusion), kind=kOutput, calls=%fused_computation.4 | convolution fusion | flops 2149056512 | bytes 19923008 | tf_op jit(solution)/shard_map/tkij,tkjf->tif/dot_general | solution.py:38
  177.0 0.0 copy-done.3
  177.0 0.0 copy-start.4
  177.0 1.6 multiply_convert_fusion.1
  178.7 0.0 copy-done.4
  178.7 2.2 fusion.6
  180.9 0.0 all-reduce.3.cloned.1.call-update
  180.9 0.0 all-reduce.5.cloned.1.call-start
  181.0 125.0 %all-reduce.3.cloned.1.call-done = f32[1024,512]{1,0:T(8,128)} async-done(((f32[1024,512]{1,0:T(8,128)}), f32[1024,512]{1,0:T(8,128)}) %all-reduce.3.cloned.1.call-update) | async-done | bytes 2097168 | tf_op jit(solution)/shard_map/psum | solution.py:46
  306.0 0.0 all-reduce.5.cloned.1.call-update
  306.0 91.2 %all-reduce.5.cloned.1.call-done = f32[1024,512]{1,0:T(8,128)} async-done(((f32[1024,512]{1,0:T(8,128)}), f32[1024,512]{1,0:T(8,128)}) %all-reduce.5.cloned.1.call-update) | async-done | bytes 2097168 | tf_op jit(solution)/shard_map/psum | solution.py:46
  397.2 3.1 copy.13
  (10 shorter events, 0.1 us)
Async XLA Ops:
  7.2 30.5 %copy-start = (bf16[512,1024]{1,0:T(8,128)(2,1)S(1)}, bf16[512,1024]{1,0:T(8,128)(2,1)}, u32[]{:S(2)}) copy-start(bf16[512,1024]{1,0:T(8,128)(2,1)} %param.7) | copy-start | bytes 3145732
  41.0 23.5 %all-to-all-start.1 = ((bf16[128,4,1024]{2,1,0:T(4,128)(2,1)}), bf16[128,4,1024]{2,1,0:T(4,128)(2,1)S(1)}, u32[]{:S(2)}, u32[]{:S(2)}) async-start(bf16[128,4,1024]{2,1,0:T(4,128)(2,1)} %reshape.72), calls=%async_computation.1 | async-start | bytes 2097152 | tf_op jit(solution)/shard_map/all_to_all | solution.py:22
  45.4 110.8 %all-gather.3.cloned.1.call-start = ((), (), s32[]{:S(2)}) async-start(), calls=%async_computation.4 | async-start | bytes 17825792 | tf_op jit(solution)/shard_map/all_gather | solution.py:33
  64.7 2.9 copy-start.2
  64.7 3.0 copy-start.5
  67.5 238.5 %all-reduce.3.cloned.1.call-start = ((), (), s32[]{:S(2)}) async-start(), calls=%async_computation.2 | async-start | bytes 4194304 | tf_op jit(solution)/shard_map/psum | solution.py:46
  156.2 13.5 %copy-start.1 = (bf16[4,16,128,128]{3,2,1,0:T(8,128)(2,1)S(1)}, bf16[4,16,128,128]{3,2,1,0:T(8,128)(2,1)}, u32[]{:S(2)}) copy-start(bf16[4,16,128,128]{3,2,1,0:T(8,128)(2,1)} %param.11) | copy-start | bytes 6291460
  169.7 7.3 %copy-start.3 = (bf16[1024,512]{1,0:T(8,128)(2,1)S(1)}, bf16[1024,512]{1,0:T(8,128)(2,1)}, u32[]{:S(2)}) copy-start(bf16[1024,512]{1,0:T(8,128)(2,1)} %param.12) | copy-start | bytes 3145732
  177.0 1.7 copy-start.4
  180.9 216.3 %all-reduce.5.cloned.1.call-start = ((), (), s32[]{:S(2)}) async-start(), calls=%async_computation.3 | async-start | bytes 4194304 | tf_op jit(solution)/shard_map/psum | solution.py:46
Sparse Core Ops, SparseCore 0:
  67.6 88.4 all-gather.2
  181.1 124.8 all-reduce.2
  308.5 88.6 all-reduce.4

commit v2 on v0

--- a/solution.py
+++ b/solution.py
@@ -30,7 +30,9 @@
     hidden_units = weight.shape[1]
     tiles_dev, blocks, tile_size, _ = block_vals.shape
     ordered = regroup(features, node_order)
-    everyone = lax.all_gather(ordered, "dom", axis=0, tiled=True)
+    everyone = jnp.concatenate(
+        lax.all_to_all(jnp.stack([ordered] * lax.axis_size("dom")), "dom", 0, 0), axis=0
+    )
     panel_tiles = everyone.reshape(-1, tile_size, width_in)
     live_mask = lax.broadcasted_iota(jnp.int32, (tiles_dev, blocks), 1) < block_count[:, None]
     masked_vals = jnp.where(live_mask[:, :, None, None], block_vals, jnp.zeros((), jnp.bfloat16))

time: 342 us -> 445 us (1.30)
  waiting for transfers between devices: 255 us -> 346 us
  starting transfers between devices: 4.48 us -> 10.6 us
  local copies, waits for them, and re-layouts: 27.2 us -> 32.6 us
    all_to_all x0 -> x1, waiting for transfers between devices: none -> 184 us  [shards(): lax.all_to_all(jnp.stack([ordered] * lax.axis_size('dom')), 'dom', 0, 0)]
    all_gather x1 -> x0, waiting for transfers between devices: 88.4 us -> none  [shards(): everyone = lax.all_gather(ordered, 'dom', axis=0, tiled=True)]
    all_to_all x0 -> x1, starting transfers between devices: none -> 6.21 us  [shards(): lax.all_to_all(jnp.stack([ordered] * lax.axis_size('dom')), 'dom', 0, 0)]
    another operation x0 -> x1, local copies, waits for them, and re-layouts: none -> 5.99 us  [shards(): jnp.stack([ordered] * lax.axis_size('dom'))]
    psum x1, waiting for transfers between devices: 151 us -> 146 us  [shards(): grad_weight = lax.psum(local_grad, ('grp', 'dom'))]
where the time goes in v2:
time: 445 us
  waiting for transfers between devices  346 us (78%)
  local copies, waits for them, and re-layouts  32.6 us (7%)
  blocking collectives  20.9 us (5%)
  between operations  14.2 us (3%)
  matrix products  11.2 us (3%)
  starting transfers between devices  10.6 us (2%)
  other arithmetic  9.24 us (2%)
    all_to_all x1, waiting for transfers between devices, shards(): lax.all_to_all(jnp.stack([ordered] * lax.axis_size('dom')), 'dom', 0, 0)  184 us
    psum x1, waiting for transfers between devices, shards(): grad_weight = lax.psum(local_grad, ('grp', 'dom'))  146 us
    all_to_all x1, blocking collectives, regroup(): lax.all_to_all(requests, ('grp', 'dom'), split_axis=0, concat_axis=0, til...  20.9 us
    all_to_all x1, waiting for transfers between devices, regroup(): lax.all_to_all(outgoing, ('grp', 'dom'), split_axis=0, concat_axis=0, til...  15.3 us
    gather x1, local copies, waits for them, and re-layouts, shards(): selected = panel_tiles[block_cols]  13.5 us
  transfers between devices with their start and end apart: 3, of which 3 were waited for; matrix products, arithmetic and copies ran while one was open for 1% of the time, Pallas kernels for 0%

profile of v2, /device:TPU:1, one launch (start us, length us, event | category | flops | bytes accessed | tf_op | source)
XLA Modules:
  0.0 444.6 jit_solution(323666849598027105)
XLA Ops:
  7.2 0.0 copy-start
  7.2 0.8 add_select_fusion
  8.0 3.8 sort.34
  11.7 3.5 gather_fusion
  15.2 0.1 all_to_all.12
  15.4 20.9 %all_to_all.19 = s32[128,1,4]{2,1,0:T(1,128)S(1)} all-to-all(s32[128,1,4]{2,1,0:T(1,128)S(1)} %bitcast.15), channel_id=1, replica_groups=mesh['grp'=8,'dom'=16] {'grp','dom'}, dimensions={0} | all-to-all | bytes 4096 | tf_op jit(solution)/shard_map/all_to_all | solution.py:20
  36.2 0.5 broadcast.78
  36.7 0.8 reduce.3
  37.6 0.1 reshape.70
  37.7 0.0 copy-done
  37.7 2.1 gather_fusion.1
  39.8 1.2 reshape.71
  41.0 4.4 all-to-all-start.1
  45.4 3.8 sort.35
  49.2 15.3 %all-to-all-done.1 = bf16[128,4,1024]{2,1,0:T(4,128)(2,1)S(1)} async-done(((bf16[128,4,1024]{2,1,0:T(4,128)(2,1)}), bf16[128,4,1024]{2,1,0:T(4,128)(2,1)S(1)}, u32[]{:S(2)}, u32[]{:S(2)}) %all-to-all-start.1) | async-done | bytes 1048608 | tf_op jit(solution)/shard_map/all_to_all | solution.py:22
  64.4 0.3 reshape.72
  64.7 2.1 gather_fusion.2
  66.8 6.0 %stack.2 = bf16[16,512,1024]{2,1,0:T(8,128)(2,1)} broadcast(bf16[512,1024]{1,0:T(8,128)(2,1)S(1)} %gather_fusion.2), dimensions={1,2} | broadcast | bytes 17825792 | tf_op jit(solution)/shard_map/stack | solution.py:34
  72.8 0.0 copy-start.3
  72.8 0.0 copy-start.6
  72.8 6.2 %all-to-all-start.2 = ((bf16[16,512,1024]{2,1,0:T(8,128)(2,1)}), bf16[16,512,1024]{2,1,0:T(8,128)(2,1)}, u32[]{:S(2)}, u32[]{:S(2)}) async-start(bf16[16,512,1024]{2,1,0:T(8,128)(2,1)} %stack.2), calls=%async_computation.2 | async-start | bytes 33554432 | tf_op jit(solution)/shard_map/all_to_all | solution.py:34
  79.0 0.0 all-reduce.2.cloned.1.call-start
  79.0 0.0 copy-done.3
  79.0 0.1 reshape.100
  79.1 0.0 copy-done.6
  79.1 0.1 iota_compare_fusion
  79.2 184.4 %all-to-all-done.2 = bf16[16,512,1024]{2,1,0:T(8,128)(2,1)} async-done(((bf16[16,512,1024]{2,1,0:T(8,128)(2,1)}), bf16[16,512,1024]{2,1,0:T(8,128)(2,1)}, u32[]{:S(2)}, u32[]{:S(2)}) %all-to-all-start.2) | async-done | bytes 16777248 | tf_op jit(solution)/shard_map/all_to_all | solution.py:34
  263.6 0.0 copy-start.2
  263.6 13.5 %gather_fusion.3 = bf16[64,128,1024]{2,1,0:T(8,128)(2,1)} fusion(bf16[64,128,1024]{2,1,0:T(8,128)(2,1)} %bitcast.2, s32[1024]{0:T(1024)S(1)} %pad_clamp_fusion), kind=kCustom, calls=%fused_computation.3 | custom fusion | bytes 33554688 | tf_op jit(solution)/shard_map/gather | solution.py:39
  277.1 0.0 copy-done.2
  277.1 0.0 copy-start.4
  277.1 7.3 %bitcast_convert_fusion = bf16[4,128,1024]{2,1,0:T(8,128)(2,1)S(1)} fusion(bf16[4,16,128,1024]{3,2,1,0:T(8,128)(2,1)} %bitcast.12, bf16[4,16,128,128]{3,2,1,0:T(8,128)(2,1)S(1)} %copy-done.2, pred[4,16]{1,0:T(4,128)(4,1)S(1)} %iota_compare_fusion), kind=kOutput, calls=%fused_computation.4 | convolution fusion | flops 2149056512 | bytes 19923008 | tf_op jit(solution)/shard_map/tkij,tkjf->tif/dot_general | solution.py:40
  284.4 0.0 copy-done.4
  284.4 0.0 copy-start.5
  284.5 1.6 multiply_convert_fusion.1
  286.1 0.0 copy-done.5
  286.1 2.2 fusion.6
  288.3 0.0 all-reduce.2.cloned.1.call-update
  288.4 146.2 %all-reduce.2.cloned.1.call-done = f32[1024,512]{1,0:T(8,128)} async-done(((f32[1024,512]{1,0:T(8,128)}), f32[1024,512]{1,0:T(8,128)}) %all-reduce.2.cloned.1.call-update) | async-done | bytes 2097168 | tf_op jit(solution)/shard_map/psum | solution.py:48
  434.6 0.0 copy-start.1
  434.6 3.2 copy.12
  437.8 0.0 copy-done.1
  (10 shorter events, 0.1 us)
Async XLA Ops:
  7.2 30.5 %copy-start = (bf16[512,1024]{1,0:T(8,128)(2,1)S(1)}, bf16[512,1024]{1,0:T(8,128)(2,1)}, u32[]{:S(2)}) copy-start(bf16[512,1024]{1,0:T(8,128)(2,1)} %param.7) | copy-start | bytes 3145732
  41.0 23.5 %all-to-all-start.1 = ((bf16[128,4,1024]{2,1,0:T(4,128)(2,1)}), bf16[128,4,1024]{2,1,0:T(4,128)(2,1)S(1)}, u32[]{:S(2)}, u32[]{:S(2)}) async-start(bf16[128,4,1024]{2,1,0:T(4,128)(2,1)} %reshape.71), calls=%async_computation.1 | async-start | bytes 2097152 | tf_op jit(solution)/shard_map/all_to_all | solution.py:22
  72.8 6.3 %copy-start.3 = (s32[4,16]{1,0:T(4,128)S(1)}, s32[4,16]{1,0:T(4,128)}, u32[]{:S(2)}) copy-start(s32[4,16]{1,0:T(4,128)} %param.9) | copy-start | bytes 772
  72.8 6.4 %copy-start.6 = (s32[4]{0:T(128)S(1)}, s32[4]{0:T(128)}, u32[]{:S(2)}) copy-start(s32[4]{0:T(128)} %param.10) | copy-start | bytes 52
  72.8 190.8 %all-to-all-start.2 = ((bf16[16,512,1024]{2,1,0:T(8,128)(2,1)}), bf16[16,512,1024]{2,1,0:T(8,128)(2,1)}, u32[]{:S(2)}, u32[]{:S(2)}) async-start(bf16[16,512,1024]{2,1,0:T(8,128)(2,1)} %stack.2), calls=%async_computation.2 | async-start | bytes 33554432 | tf_op jit(solution)/shard_map/all_to_all | solution.py:34
  79.0 355.6 %all-reduce.2.cloned.1.call-start = ((), (), s32[]{:S(2)}) async-start(), calls=%async_computation.3 | async-start | bytes 4194304 | tf_op jit(solution)/shard_map/psum | solution.py:48
  263.6 13.5 %copy-start.2 = (bf16[4,16,128,128]{3,2,1,0:T(8,128)(2,1)S(1)}, bf16[4,16,128,128]{3,2,1,0:T(8,128)(2,1)}, u32[]{:S(2)}) copy-start(bf16[4,16,128,128]{3,2,1,0:T(8,128)(2,1)} %param.11) | copy-start | bytes 6291460
  277.1 7.3 %copy-start.4 = (bf16[1024,512]{1,0:T(8,128)(2,1)S(1)}, bf16[1024,512]{1,0:T(8,128)(2,1)}, u32[]{:S(2)}) copy-start(bf16[1024,512]{1,0:T(8,128)(2,1)} %param.12) | copy-start | bytes 3145732
  284.4 1.7 copy-start.5
  434.6 3.2 copy-start.1
Sparse Core Ops, SparseCore 0:
  288.5 146.0 all-reduce.1
